TPU v7x, 512 devices: a whole 4x4x16 slice. The times are simulated.
512 devices in a mesh: sample: 32 (over x, y, core), cls: 16 (over z).
Axes of the slice: x: 4, y: 4, z: 16, core: 2. Of those that a mesh axis runs over, the one named last changes fastest.
Arguments:
- features: bfloat16 [16384, 2048], P('sample', 'cls'), may hold values from -1.5 to 1.5
- head: bfloat16 [2048, 8192], P('sample', 'cls'), may hold values from -1.5859375 to 1.5859375
- class_cap: bfloat16 [8192], P('cls'), may hold values from 0.5 to 4
Outputs:
- targets: bfloat16 [16384, 8192], P('sample', 'cls')
- grad_features: bfloat16 [16384, 2048], P('sample', 'cls')
- grad_head: bfloat16 [2048, 8192], P('sample', 'cls')
All inputs are finite; a program needn't handle non-finite values.
Results may differ from a plain program's by a relative error of at most 0.02.
Values may be sent and summed in bfloat16 or wider, within the bound.
A program may use at most 64 MiB of HBM per device.

v0:
```python
import jax
import jax.numpy as jnp
from jax import lax
from jax.sharding import PartitionSpec as P

ITERS = 3
softcap = 15.0
sharpen = 2.0


def row_total(values):
    return lax.psum(jnp.sum(values, axis=1), "cls")


def per_device(features, head, class_cap):
    local_rows = features.shape[0]
    class_local = head.shape[1]
    sample_count = lax.axis_size("sample")
    class_groups = lax.axis_size("cls")
    ratio = local_rows * sample_count / (class_local * class_groups)
    whole = lax.all_gather(features, "cls", axis=1, tiled=True)
    head_full = lax.all_gather(head, "sample", axis=0, tiled=True)
    logits = jnp.dot(whole, head_full, preferred_element_type=jnp.float32)
    capped = softcap * jnp.tanh(logits / softcap)
    student = jnp.exp(capped)
    transport = jnp.exp(capped * sharpen)
    student_mass, plan_mass = lax.psum(
        (jnp.sum(student, axis=1), jnp.sum(transport, axis=1)), "cls"
    )
    student = student / student_mass[:, None]
    ceiling = class_cap.astype(jnp.float32) * ratio
    for iteration in range(ITERS):
        if iteration > 0:
            plan_mass = row_total(transport)
        transport = transport / plan_mass[:, None]
        column_mass = lax.psum(jnp.sum(transport, axis=0), "sample")
        transport = transport * jnp.minimum(1.0, ceiling / column_mass)
    targets = (transport / row_total(transport)[:, None]).astype(jnp.bfloat16)
    tanh_slope = 1.0 - (capped / softcap) ** 2
    grad_logits = ((student - targets.astype(jnp.float32)) * tanh_slope).astype(jnp.bfloat16)
    grad_head = lax.psum_scatter(
        lax.dot_general(
            whole, grad_logits, (((0,), (0,)), ((), ())), preferred_element_type=jnp.float32
        ).astype(jnp.bfloat16),
        "sample",
        scatter_dimension=0,
        tiled=True,
    )
    share = lax.psum_scatter(
        lax.dot_general(
            head_full, grad_logits, (((1,), (1,)), ((), ())), preferred_element_type=jnp.float32
        ).astype(jnp.bfloat16),
        "cls",
        scatter_dimension=0,
        tiled=True,
    ).astype(jnp.float32)
    grad_features = jnp.transpose(share).astype(jnp.bfloat16)
    return (targets, grad_features, grad_head)


def solution(mesh):
    return jax.shard_map(
        per_device,
        mesh=mesh,
        in_specs=(P("sample", "cls"), P("sample", "cls"), P("cls")),
        out_specs=(P("sample", "cls"), P("sample", "cls"), P("sample", "cls")),
        check_vma=False,
    )
```

profile of v0, /device:TPU:2, one launch (start us, length us, event | category | flops | bytes accessed | tf_op | source)
XLA Modules:
  0.0 643.5 jit_solution(15477664846677126857)
XLA Ops:
  7.2 0.0 all-gather.3.cloned.1.call-start
  7.2 0.7 all-gather.3.cloned.1.call-update
  7.9 0.0 all-gather.5.cloned.1.call-start
  7.9 0.7 all-gather.5.cloned.1.call-update
  8.6 0.0 copy-start
  8.7 0.0 reduce-scatter.7.cloned.1.call-start
  8.7 85.0 %all-gather.3.cloned.1.call-done = bf16[512,2048]{1,0:T(8,128)(2,1)} async-done(((bf16[512,128]{1,0:T(8,128)(2,1)}), bf16[512,2048]{1,0:T(8,128)(2,1)}) %all-gather.3.cloned.1.call-update) | async-done | bytes 2097168 | tf_op jit(solution)/shard_map/all_gather | solution.py:21
  93.7 57.1 %all-gather.5.cloned.1.call-done = bf16[2048,512]{1,0:T(8,128)(2,1)} async-done(((bf16[64,512]{1,0:T(8,128)(2,1)}), bf16[2048,512]{1,0:T(8,128)(2,1)}) %all-gather.5.cloned.1.call-update) | async-done | bytes 2097168 | tf_op jit(solution)/shard_map/all_gather | solution.py:22
  150.9 3.7 fusion.5
  154.6 31.3 %psum.56 = f32[512]{0:T(512)S(1)} all-reduce(f32[512]{0:T(512)S(1)} %get-tuple-element.17), channel_id=1, replica_groups=mesh['sample'=32,'cls'=16] {'cls'}, use_global_device_ids=true, to_apply=%region_1.0 | all-reduce | flops 512 | bytes 4096 | tf_op jit(solution)/shard_map/psum | solution.py:27
  185.8 0.3 fusion.12
  186.1 53.0 %psum.57 = f32[512]{0:T(512)S(1)} all-reduce(f32[512]{0:T(512)S(1)} %fusion.12), channel_id=1, replica_groups=mesh['sample'=32,'cls'=16] {'sample'}, use_global_device_ids=true, to_apply=%region_3.0 | all-reduce | flops 512 | bytes 4096 | tf_op jit(solution)/shard_map/psum | solution.py:36
  239.1 0.0 copy-done
  239.1 0.4 fusion.3
  239.5 28.4 %psum.58 = f32[512]{0:T(512)S(1)} all-reduce(f32[512]{0:T(512)S(1)} %get-tuple-element.10), channel_id=1, replica_groups=mesh['sample'=32,'cls'=16] {'cls'}, use_global_device_ids=true, to_apply=%region_5.0 | all-reduce | flops 512 | bytes 4096 | tf_op jit(solution)/shard_map/psum | solution.py:12
  267.8 0.3 fusion.14
  268.2 55.0 %psum.59 = f32[512]{0:T(512)S(1)} all-reduce(f32[512]{0:T(512)S(1)} %get-tuple-element.15), channel_id=1, replica_groups=mesh['sample'=32,'cls'=16] {'sample'}, use_global_device_ids=true, to_apply=%region_7.0 | all-reduce | flops 512 | bytes 4096 | tf_op jit(solution)/shard_map/psum | solution.py:36
  323.2 0.2 multiply_reduce_fusion.1
  323.4 28.9 %psum.60 = f32[512]{0:T(512)S(1)} all-reduce(f32[512]{0:T(512)S(1)} %multiply_reduce_fusion.1), channel_id=1, replica_groups=mesh['sample'=32,'cls'=16] {'cls'}, use_global_device_ids=true, to_apply=%region_9.0 | all-reduce | flops 512 | bytes 4096 | tf_op jit(solution)/shard_map/psum | solution.py:12
  352.2 0.3 fusion.13
  352.5 62.7 %psum.61 = f32[512]{0:T(512)S(1)} all-reduce(f32[512]{0:T(512)S(1)} %fusion.13), channel_id=1, replica_groups=mesh['sample'=32,'cls'=16] {'sample'}, use_global_device_ids=true, to_apply=%region_11.0 | all-reduce | flops 512 | bytes 4096 | tf_op jit(solution)/shard_map/psum | solution.py:36
  415.2 0.2 multiply_reduce_fusion
  415.4 27.9 %all-reduce = (f32[512]{0:T(512)S(1)}, f32[512]{0:T(512)S(1)}) all-reduce(f32[512]{0:T(512)S(1)} %multiply_reduce_fusion, f32[512]{0:T(512)S(1)} %get-tuple-element.9), channel_id=1, replica_groups=mesh['sample'=32,'cls'=16] {'cls'}, use_global_device_ids=true, to_apply=%region_13.0 | all-reduce | flops 1024 | bytes 8192 | tf_op jit(solution)/shard_map/psum | solution.py:12
  443.3 0.0 copy-start.1
  443.3 0.5 multiply_convert_fusion
  443.8 1.1 copy-done.1
  444.9 1.3 fusion
  446.2 2.6 copy.10
  448.8 0.0 reduce-scatter.7.cloned.1.call-update
  448.8 0.0 reduce-scatter.9.cloned.1.call-start
  448.8 2.8 fusion.1
  451.7 2.5 copy.12
  454.2 0.0 reduce-scatter.9.cloned.1.call-update
  454.2 1.0 copy.8
  455.2 77.6 %reduce-scatter.7.cloned.1.call-done = bf16[128,512]{1,0:T(8,128)(2,1)} async-done(((bf16[2048,512]{1,0:T(8,128)(2,1)}), bf16[128,512]{1,0:T(8,128)(2,1)}) %reduce-scatter.7.cloned.1.call-update) | async-done | bytes 131088
  532.9 1.7 copy.11
  534.5 102.4 %reduce-scatter.9.cloned.1.call-done = bf16[64,512]{1,0:T(8,128)(2,1)} async-done(((bf16[2048,512]{1,0:T(8,128)(2,1)}), bf16[64,512]{1,0:T(8,128)(2,1)}) %reduce-scatter.9.cloned.1.call-update) | async-done | bytes 65552
  (3 shorter events, 0.0 us)
Async XLA Ops:
  7.2 86.6 %all-gather.3.cloned.1.call-start = ((), (), s32[]{:S(2)}) async-start(), calls=%async_computation.2 | async-start | bytes 2228224 | tf_op jit(solution)/shard_map/all_gather | solution.py:21
  7.9 143.0 %all-gather.5.cloned.1.call-start = ((), (), s32[]{:S(2)}) async-start(), calls=%async_computation.3 | async-start | bytes 2162688 | tf_op jit(solution)/shard_map/all_gather | solution.py:22
  8.6 230.4 %copy-start = (bf16[512]{0:T(512)(128)(2,1)S(1)}, bf16[512]{0:T(512)(128)(2,1)}, u32[]{:S(2)}) copy-start(bf16[512]{0:T(512)(128)(2,1)} %param.5) | copy-start | bytes 3076
  8.7 524.2 %reduce-scatter.7.cloned.1.call-start = ((), (), s32[]{:S(2)}) async-start(), calls=%async_computation.4 | async-start | bytes 2228224
  443.3 1.6 copy-start.1
  448.8 188.2 %reduce-scatter.9.cloned.1.call-start = ((), (), s32[]{:S(2)}) async-start(), calls=%async_computation.5 | async-start | bytes 2162688
Sparse Core Ops, SparseCore 0:
  10.0 83.7 all-gather.2
  96.9 53.9 all-gather.4
  448.9 83.9 reduce-scatter.6
  537.7 99.1 reduce-scatter.8
where the time goes:
time: 644 us; the launch traced here: 643 us
  waiting for transfers between devices  324 us (50%)
  blocking collectives  287 us (45%)
  between operations  13.8 us (2%)
  local copies, waits for them, and re-layouts  8.86 us (1%)
  matrix products  7.84 us (1%)
    unnamed x6, waiting for transfers between devices  181 us
    psum x3, blocking collectives, per_device(): column_mass = lax.psum(jnp.sum(transport, axis=0), 'sample')  171 us
    psum x3, blocking collectives, row_total(): return lax.psum(jnp.sum(values, axis=1), 'cls')  85.2 us
    all_gather x1, waiting for transfers between devices, per_device(): whole = lax.all_gather(features, 'cls', axis=1, tiled=True)  85 us
    all_gather x1, waiting for transfers between devices, per_device(): head_full = lax.all_gather(head, 'sample', axis=0, tiled=True)  57.1 us
    psum x1, blocking collectives, per_device(): lax.psum((jnp.sum(student, axis=1), jnp.sum(transport, axis=1)), 'cls')  31.3 us
  transfers between devices with their start and end apart: 4, of which 4 were waited for; matrix products, arithmetic and copies ran while one was open for 1% of the time, Pallas kernels for 0%

commit v1 on v0

--- a/solution.py
+++ b/solution.py
@@ -1,3 +1,4 @@
+import functools
 import jax
 import jax.numpy as jnp
 from jax import lax
@@ -8,8 +9,15 @@
 sharpen = 2.0
 
 
+def balance_sample_on(body, along_axis):
+    return jnp.sum(jax.lax.all_gather(body, along_axis), 0)
+
+
+put_the_ends = functools.partial(balance_sample_on, along_axis="cls")
+
+
 def row_total(values):
-    return lax.psum(jnp.sum(values, axis=1), "cls")
+    return put_the_ends(jnp.sum(values, axis=1))
 
 
 def per_device(features, head, class_cap):

time: 644 us -> 669 us (1.039)
  blocking collectives: 287 us -> 312 us
    psum x3 -> x0, blocking collectives: 85.2 us -> none  [row_total(): return lax.psum(jnp.sum(values, axis=1), 'cls')]
    all_gather x0 -> x3, blocking collectives: none -> 82.1 us  [balance_sample_on(): return jnp.sum(jax.lax.all_gather(body, along_axis), 0)]
    psum x1 -> x2, blocking collectives: 31.3 us -> 59.7 us  [per_device(): lax.psum((jnp.sum(student, axis=1), jnp.sum(transport, axis=1)), 'cls')]
where the time goes in v1:
time: 669 us
  waiting for transfers between devices  323 us (48%)
  blocking collectives  312 us (47%)
  between operations  13.8 us (2%)
  local copies, waits for them, and re-layouts  8.86 us (1%)
  matrix products  7.85 us (1%)
    unnamed x6, waiting for transfers between devices  181 us
    psum x3, blocking collectives, per_device(): column_mass = lax.psum(jnp.sum(transport, axis=0), 'sample')  171 us
    all_gather x1, waiting for transfers between devices, per_device(): whole = lax.all_gather(features, 'cls', axis=1, tiled=True)  85 us
    all_gather x3, blocking collectives, balance_sample_on(): return jnp.sum(jax.lax.all_gather(body, along_axis), 0)  82.1 us
    psum x2, blocking collectives, per_device(): lax.psum((jnp.sum(student, axis=1), jnp.sum(transport, axis=1)), 'cls')  59.7 us
    all_gather x1, waiting for transfers between devices, per_device(): head_full = lax.all_gather(head, 'sample', axis=0, tiled=True)  57.1 us
  transfers between devices with their start and end apart: 4, of which 4 were waited for; matrix products, arithmetic and copies ran while one was open for 1% of the time, Pallas kernels for 0%

profile of v1, /device:TPU:2, one launch (start us, length us, event | category | flops | bytes accessed | tf_op | source)
XLA Modules:
  0.0 668.5 jit_solution(9500383681080833258)
XLA Ops:
  7.2 0.0 all-gather.9.cloned.1.call-start
  7.2 0.7 all-gather.9.cloned.1.call-update
  7.9 0.0 all-gather.11.cloned.1.call-start
  7.9 0.7 all-gather.11.cloned.1.call-update
  8.6 0.0 copy-start
  8.7 0.0 reduce-scatter.7.cloned.1.call-start
  8.7 85.0 %all-gather.9.cloned.1.call-done = bf16[512,2048]{1,0:T(8,128)(2,1)} async-done(((bf16[512,128]{1,0:T(8,128)(2,1)}), bf16[512,2048]{1,0:T(8,128)(2,1)}) %all-gather.9.cloned.1.call-update) | async-done | bytes 2097168 | tf_op jit(solution)/shard_map/all_gather | solution.py:29
  93.7 57.1 %all-gather.11.cloned.1.call-done = bf16[2048,512]{1,0:T(8,128)(2,1)} async-done(((bf16[64,512]{1,0:T(8,128)(2,1)}), bf16[2048,512]{1,0:T(8,128)(2,1)}) %all-gather.11.cloned.1.call-update) | async-done | bytes 2097168 | tf_op jit(solution)/shard_map/all_gather | solution.py:30
  150.9 3.7 fusion.5
  154.6 31.3 %psum.35 = f32[512]{0:T(512)S(1)} all-reduce(f32[512]{0:T(512)S(1)} %get-tuple-element.15), channel_id=1, replica_groups=mesh['sample'=32,'cls'=16] {'cls'}, use_global_device_ids=true, to_apply=%region_1.0 | all-reduce | flops 512 | bytes 4096 | tf_op jit(solution)/shard_map/psum | solution.py:35
  185.8 0.3 fusion.12
  186.1 53.0 %psum.36 = f32[512]{0:T(512)S(1)} all-reduce(f32[512]{0:T(512)S(1)} %fusion.12), channel_id=1, replica_groups=mesh['sample'=32,'cls'=16] {'sample'}, use_global_device_ids=true, to_apply=%region_3.0 | all-reduce | flops 512 | bytes 4096 | tf_op jit(solution)/shard_map/psum | solution.py:44
  239.1 0.0 copy-done
  239.1 0.4 fusion.3
  239.5 28.4 %psum.39 = f32[512]{0:T(512)S(1)} all-reduce(f32[512]{0:T(512)S(1)} %get-tuple-element.9), channel_id=1, replica_groups=mesh['sample'=32,'cls'=16] {'cls'}, use_global_device_ids=true, to_apply=%region_15.0 | all-reduce | flops 512 | bytes 4096 | tf_op jit(solution)/shard_map/psum | solution.py:35
  267.8 27.9 %all-gather.3 = f32[16,1,512]{2,1,0:T(1,128)S(1)} all-gather(f32[1,1,512]{2,1,0:T(1,128)S(1)} %bitcast.17), channel_id=2, replica_groups=mesh['sample'=32,'cls'=16] {'cls'}, dimensions={0}, use_global_device_ids=true | all-gather | bytes 34816 | tf_op jit(solution)/shard_map/all_gather | solution.py:13
  295.8 0.3 fusion.14
  296.2 55.0 %psum.37 = f32[512]{0:T(512)S(1)} all-reduce(f32[512]{0:T(512)S(1)} %get-tuple-element.13), channel_id=1, replica_groups=mesh['sample'=32,'cls'=16] {'sample'}, use_global_device_ids=true, to_apply=%region_7.0 | all-reduce | flops 512 | bytes 4096 | tf_op jit(solution)/shard_map/psum | solution.py:44
  351.2 0.2 multiply_reduce_fusion.1
  351.3 26.9 %all-gather.4 = f32[16,1,512]{2,1,0:T(1,128)S(1)} all-gather(f32[1,1,512]{2,1,0:T(1,128)S(1)} %bitcast.18), channel_id=3, replica_groups=mesh['sample'=32,'cls'=16] {'cls'}, dimensions={0}, use_global_device_ids=true | all-gather | bytes 34816 | tf_op jit(solution)/shard_map/all_gather | solution.py:13
  378.3 0.3 fusion.13
  378.6 62.7 %psum.38 = f32[512]{0:T(512)S(1)} all-reduce(f32[512]{0:T(512)S(1)} %fusion.13), channel_id=1, replica_groups=mesh['sample'=32,'cls'=16] {'sample'}, use_global_device_ids=true, to_apply=%region_11.0 | all-reduce | flops 512 | bytes 4096 | tf_op jit(solution)/shard_map/psum | solution.py:44
  441.3 0.2 multiply_reduce_fusion
  441.5 27.2 %all-gather.5 = f32[16,1,512]{2,1,0:T(1,128)S(1)} all-gather(f32[1,1,512]{2,1,0:T(1,128)S(1)} %bitcast.19), channel_id=4, replica_groups=mesh['sample'=32,'cls'=16] {'cls'}, dimensions={0}, use_global_device_ids=true | all-gather | bytes 34816 | tf_op jit(solution)/shard_map/all_gather | solution.py:13
  468.7 0.0 copy-start.1
  468.7 0.5 multiply_convert_fusion
  469.2 1.1 copy-done.1
  470.3 1.3 fusion
  471.7 2.6 copy.10
  474.2 0.0 reduce-scatter.7.cloned.1.call-update
  474.2 0.0 reduce-scatter.9.cloned.1.call-start
  474.3 2.8 fusion.1
  477.1 2.5 copy.12
  479.7 0.0 reduce-scatter.9.cloned.1.call-update
  479.7 1.0 copy.8
  480.7 77.1 %reduce-scatter.7.cloned.1.call-done = bf16[128,512]{1,0:T(8,128)(2,1)} async-done(((bf16[2048,512]{1,0:T(8,128)(2,1)}), bf16[128,512]{1,0:T(8,128)(2,1)}) %reduce-scatter.7.cloned.1.call-update) | async-done | bytes 131088
  557.8 1.7 copy.11
  559.5 102.5 %reduce-scatter.9.cloned.1.call-done = bf16[64,512]{1,0:T(8,128)(2,1)} async-done(((bf16[2048,512]{1,0:T(8,128)(2,1)}), bf16[64,512]{1,0:T(8,128)(2,1)}) %reduce-scatter.9.cloned.1.call-update) | async-done | bytes 65552
  (6 shorter events, 0.2 us)
Async XLA Ops:
  7.2 86.6 %all-gather.9.cloned.1.call-start = ((), (), s32[]{:S(2)}) async-start(), calls=%async_computation.2 | async-start | bytes 2228224 | tf_op jit(solution)/shard_map/all_gather | solution.py:29
  7.9 143.0 %all-gather.11.cloned.1.call-start = ((), (), s32[]{:S(2)}) async-start(), calls=%async_computation.3 | async-start | bytes 2162688 | tf_op jit(solution)/shard_map/all_gather | solution.py:30
  8.6 230.4 %copy-start = (bf16[512]{0:T(512)(128)(2,1)S(1)}, bf16[512]{0:T(512)(128)(2,1)}, u32[]{:S(2)}) copy-start(bf16[512]{0:T(512)(128)(2,1)} %param.5) | copy-start | bytes 3076
  8.7 549.2 %reduce-scatter.7.cloned.1.call-start = ((), (), s32[]{:S(2)}) async-start(), calls=%async_computation.4 | async-start | bytes 2228224
  468.7 1.6 copy-start.1
  474.2 187.7 %reduce-scatter.9.cloned.1.call-start = ((), (), s32[]{:S(2)}) async-start(), calls=%async_computation.5 | async-start | bytes 2162688
Sparse Core Ops, SparseCore 0:
  10.0 83.7 all-gather.8
  96.9 53.9 all-gather.10
  474.4 83.4 reduce-scatter.6
  562.7 99.2 reduce-scatter.8
